TPU v7x, 32 devices: a whole 2x2x4 slice. The times are simulated.
32 devices in a mesh: los: 8 (over z, x), sky: 4 (over y, core).
Axes of the slice: x: 2, y: 2, z: 4, core: 2. Of those that a mesh axis runs over, the one named last changes fastest.
Arguments:
- potentials: bfloat16 [32, 64, 4096], P('los', 'sky'), may hold values from -6 to 6
- shell_weight: float32 [32], P('los'), may hold values from 0.004 to 0.02
- shell_dist: float32 [32], P('los'), may hold values from 1 to 2.28, as said below
- source_dist: float32 [32], P('los'), may hold values from 1 to 2.28, as said below
Outputs:
- convergence: bfloat16 [32, 64, 4096], P('los', 'sky')
- shear_one: bfloat16 [32, 64, 4096], P('los', 'sky')
- shear_two: bfloat16 [32, 64, 4096], P('los', 'sky')
Inputs may be any that keep to these rules, and one draw needn't show every extreme that they name: shell_dist rises strictly with the shell index. source_dist[s] lies strictly between shell_dist[s] and shell_dist[s + 1].
All inputs are finite; a program needn't handle non-finite values.
Results may differ from a plain program's by a relative error of at most 0.001.
Values may be sent and summed in bfloat16 or wider, within the bound.
A program may use at most 64 MiB of HBM per device.

v0:
```python
import jax
import jax.numpy as jnp
from jax import lax
from jax.sharding import PartitionSpec as P


def with_halo(cells, sides, width):
    for axis, dim in sides:
        count = lax.axis_size(axis)
        head = lax.slice_in_dim(cells, 0, width, axis=dim)
        tail = lax.slice_in_dim(cells, cells.shape[dim] - width, cells.shape[dim], axis=dim)
        cells = jnp.concatenate(
            [
                lax.ppermute(tail, axis, [(i, (i + 1) % count) for i in range(count)]),
                cells,
                lax.ppermute(head, axis, [((i + 1) % count, i) for i in range(count)]),
            ],
            axis=dim,
        )
    return cells


def first_cols(field):
    return (
        jnp.roll(field, 2, axis=-1)
        - 8.0 * jnp.roll(field, 1, axis=-1)
        + 8.0 * jnp.roll(field, -1, axis=-1)
        - jnp.roll(field, -2, axis=-1)
    ) / 12.0


def second_cols(field):
    return (
        -jnp.roll(field, 2, axis=-1)
        + 16.0 * jnp.roll(field, 1, axis=-1)
        - 30.0 * field
        + 16.0 * jnp.roll(field, -1, axis=-1)
        - jnp.roll(field, -2, axis=-1)
    ) / 12.0


def first_rows(padded, height):
    return (
        padded[:, 0:height, :]
        - 8.0 * padded[:, 1 : height + 1, :]
        + 8.0 * padded[:, 3 : height + 3, :]
        - padded[:, 4 : height + 4, :]
    ) / 12.0


def second_rows(padded, height):
    return (
        -padded[:, 0:height, :]
        + 16.0 * padded[:, 1 : height + 1, :]
        - 30.0 * padded[:, 2 : height + 2, :]
        + 16.0 * padded[:, 3 : height + 3, :]
        - padded[:, 4 : height + 4, :]
    ) / 12.0


def local_sums(potential, near_weight, far_weight):
    field = potential.astype(jnp.float32)
    local_near = jnp.cumsum(near_weight[:, None, None] * field, axis=0)
    local_far = jnp.cumsum(far_weight[:, None, None] * field, axis=0)
    return (local_near, local_far)


def nearer_sums(total_near, total_far):
    stacked = jnp.stack((total_near, total_far))[None]
    received = lax.all_to_all(stacked, "los", split_axis=3, concat_axis=0, tiled=True)
    earlier = jnp.cumsum(received, axis=0) - received
    result = lax.all_to_all(earlier, "los", split_axis=0, concat_axis=3, tiled=True)
    return (result[0, 0], result[0, 1])


def lens_from(local_near, local_far, prefix, source_dist):
    running_near = prefix[0][None] + local_near
    running_far = prefix[1][None] + local_far
    return running_near - running_far / source_dist[:, None, None]


def on_device(potentials, shell_weight, shell_dist, source_dist):
    height = potentials.shape[1]
    near_weight = shell_weight * shell_dist
    far_weight = near_weight * shell_dist
    local_near, local_far = local_sums(potentials, near_weight, far_weight)
    prefix = nearer_sums(local_near[-1], local_far[-1])
    lens_map = lens_from(local_near, local_far, prefix, source_dist)
    padded = with_halo(lens_map, (("sky", 1),), 2)
    interior = padded[:, 2 : height + 2, :]
    second_x = second_cols(interior)
    second_y = second_rows(padded, height)
    cross = first_rows(first_cols(padded), height)
    convergence = (0.5 * (second_x + second_y)).astype(jnp.bfloat16)
    shear_one = (0.5 * (second_x - second_y)).astype(jnp.bfloat16)
    shear_two = cross.astype(jnp.bfloat16)
    return (convergence, shear_one, shear_two)


def solution(mesh):
    return jax.shard_map(
        on_device,
        mesh=mesh,
        in_specs=(P("los", "sky", None), P("los"), P("los"), P("los")),
        out_specs=(P("los", "sky", None), P("los", "sky", None), P("los", "sky", None)),
        check_vma=False,
    )
```

profile of v0, /device:TPU:0, one launch (start us, length us, event | category | flops | bytes accessed | tf_op | source)
XLA Modules:
  0.0 90.6 jit_solution(15594360975556219403)
XLA Ops:
  0.6 0.7 fusion.27
  1.4 1.2 %fusion.2 = f32[4,16,4096]{2,1,0:T(8,128)S(1)} fusion(bf16[4,16,4096]{2,1,0:T(8,128)(2,1)} %param.4, f32[4]{0:T(128)S(1)} %get-tuple-element.18), kind=kOutput, calls=%fused_computation.16 | output fusion | flops 1310720 | bytes 1572880 | tf_op jit(solution)/shard_map/jit(cumsum)/reduce_window_sum | solution.py:64
  2.9 4.4 %copy.82 = f32[1,2,16,4096]{2,1,0,3:T(2,128)} copy(f32[1,2,16,4096]{3,2,1,0:T(8,128)S(1)} %maximum_bitcast_fusion) | data formatting | bytes 1048576 | tf_op jit(solution)/shard_map/broadcast_in_dim | solution.py:69
  7.2 7.2 %reshape.11 = f32[8,1,16384]{2,1,0:T(1,128)S(1)} reshape(f32[4096,1,2,16]{3,2,1,0:T(2,128)} %bitcast.19) | data formatting | bytes 1048576
  14.5 21.6 %all_to_all.36 = f32[8,1,16384]{2,1,0:T(1,128)S(1)} all-to-all(f32[8,1,16384]{2,1,0:T(1,128)S(1)} %reshape.11), channel_id=1, replica_groups=mesh['los'=8,'sky'=4] {'los'}, dimensions={0} | all-to-all | bytes 1048576 | tf_op jit(solution)/shard_map/all_to_all | solution.py:70
  36.1 0.5 broadcast.48
  36.6 1.9 %reduce = f32[8,16384]{1,0:T(8,128)S(1)} reduce(f32[8,1,16384]{2,1,0:T(1,128)S(1)} %all_to_all.36, f32[]{:T(128)} %broadcast.48), dimensions={1}, to_apply=%all_to_all.26.reduce_sub_computation | reduce | bytes 1048580 | tf_op jit(solution)/shard_map/all_to_all | solution.py:70
  38.5 7.5 %reshape.12 = f32[4096,1,2,16]{3,2,1,0:T(2,128)} reshape(f32[8,16384]{1,0:T(8,128)S(1)} %reduce) | data formatting | bytes 1048576
  46.0 5.1 %copy.83 = f32[1,2,16,8,512]{4,2,1,3,0:T(8,128)S(1)} copy(f32[1,2,16,8,512]{2,1,4,3,0:T(2,128)} %bitcast.20) | data formatting | bytes 1048576 | tf_op jit(solution)/shard_map/all_to_all | solution.py:70
  51.1 2.4 %reduce-window_subtract_fusion = f32[8,2,16,512]{3,2,1,0:T(8,128)S(1)} fusion(f32[1,2,16,8,512]{4,2,1,3,0:T(8,128)S(1)} %copy.83), kind=kOutput, calls=%fused_computation.14 | output fusion | flops 1048576 | bytes 1048576 | tf_op jit(solution)/shard_map/jit(cumsum)/reduce_window_sum | solution.py:71
  53.5 17.5 %all_to_all.37 = f32[8,2,16,512]{3,2,1,0:T(8,128)S(1)} all-to-all(f32[8,2,16,512]{3,2,1,0:T(8,128)S(1)} %reduce-window_subtract_fusion), channel_id=1, replica_groups=mesh['los'=8,'sky'=4] {'los'}, dimensions={0} | all-to-all | bytes 1048576 | tf_op jit(solution)/shard_map/all_to_all | solution.py:72
  71.2 0.6 copy-done.1
  72.2 0.4 fusion.33
  72.6 0.4 fusion.35
  73.2 0.7 collective-permute-start
  74.0 5.0 %collective-permute-done = f32[4,2,4096]{2,0,1:T(4,128)S(1)} collective-permute-done((f32[4,2,4096]{2,0,1:T(4,128)S(1)}, f32[4,2,4096]{2,0,1:T(4,128)S(1)}, u32[]{:S(2)}, u32[]{:S(2)}) %collective-permute-start) | collective-permute-done | bytes 131104 | tf_op jit(solution)/shard_map/ppermute | solution.py:14
  79.0 0.7 copy_dynamic-update-slice_fusion
  79.8 0.8 fusion.31
  80.7 0.8 fusion.28
  81.9 1.8 %maximum_subtract_fusion = (f32[4,20,4096]{2,0,1:T(4,128)S(1)}, f32[4,20,4096]{2,0,1:T(4,128)S(1)}) fusion(f32[4,20,4094]{2,0,1:T(4,128)S(1)} %get-tuple-element.26, f32[4,20,2]{2,0,1:T(4,128)S(1)} %get-tuple-element.24, f32[4,20,4095]{2,0,1:T(4,128)S(1)} %get-tuple-element.21, f32[4,20,1]{2,0,1:T(4,128)S(1)} %get-tuple-element.23, ...), kind=kLoop, calls=%fused_computation.10 | loop fusion | flops 1638400 | bytes 6553600 | tf_op jit(solution)/shard_map/sub | solution.py:25
  83.7 2.3 %fusion = f32[4,20,4096]{2,1,0:T(8,128)S(1)} fusion(f32[4,20,4096]{2,0,1:T(4,128)S(1)} %get-tuple-element.41, f32[4,20,4096]{2,0,1:T(4,128)S(1)} %get-tuple-element.40, f32[4,20,4096]{2,0,1:T(4,128)S(1)} %pad_maximum_fusion), kind=kLoop, calls=%fused_computation.5 | loop fusion | flops 1310720 | bytes 5242880 | tf_op jit(solution)/shard_map/div | solution.py:24
  86.0 1.2 %fusion.13 = bf16[4,16,4096]{2,1,0:T(8,128)(2,1)} fusion(f32[4,20,4096]{2,1,0:T(8,128)S(1)} %fusion), kind=kLoop, calls=%fused_computation.28 | loop fusion | flops 1835008 | bytes 4718592 | tf_op jit(solution)/shard_map/convert_element_type | solution.py:96
  87.4 2.3 %multiply_convert_fusion = (bf16[4,16,4096]{2,1,0:T(8,128)(2,1)}, f32[4,16,4096]{2,1,0:T(8,128)S(1)}, f32[4,16,4096]{2,1,0:T(8,128)S(1)}) fusion(f32[4,2,4096]{2,1,0:T(2,128)S(1)} %copy.88, f32[4,16,4096]{2,1,0:T(8,128)S(1)} %divide_subtract_fusion, f32[4,2,4096]{2,1,0:T(2,128)S(1)} %copy.86, f32[4,16,2]{2,1,0:T(8,128)S(1)} %get-tuple-element.29, ...), kind=kLoop, calls=%fused_computation.45 | loop fusion | flops 7340032 | bytes 8126464 | tf_op jit(solution)/shard_map/convert_element_type | solution.py:95
  89.7 0.9 multiply_convert_fusion.1
  (24 shorter events, 1.9 us)
Async XLA Ops:
  0.6 2.0 %copy-start = (bf16[4,16,4096]{2,1,0:T(8,128)(2,1)S(1)}, bf16[4,16,4096]{2,1,0:T(8,128)(2,1)}, u32[]{:S(2)}) copy-start(bf16[4,16,4096]{2,1,0:T(8,128)(2,1)} %param.4) | copy-start | bytes 1572868
  71.1 0.7 copy-start.1
  73.0 6.7 %collective-permute-start.1 = (f32[4,2,4096]{2,0,1:T(4,128)S(1)}, f32[4,2,4096]{2,0,1:T(4,128)S(1)}, u32[]{:S(2)}, u32[]{:S(2)}) collective-permute-start(f32[4,2,4096]{2,0,1:T(4,128)S(1)} %copy.87), channel_id=1, source_target_pairs={{1,0},{2,1},{3,2},{0,3},{5,4},{6,5},{7,6},{4,7},{9,8},{10,9},{11,1... | collective-permute-start | bytes 393224 | tf_op jit(solution)/shard_map/ppermute | solution.py:16
  73.2 5.8 %collective-permute-start = (f32[4,2,4096]{2,0,1:T(4,128)S(1)}, f32[4,2,4096]{2,0,1:T(4,128)S(1)}, u32[]{:S(2)}, u32[]{:S(2)}) collective-permute-start(f32[4,2,4096]{2,0,1:T(4,128)S(1)} %copy.85), channel_id=1, source_target_pairs={{0,1},{1,2},{2,3},{3,0},{4,5},{5,6},{6,7},{7,4},{8,9},{9,10},{10,1... | collective-permute-start | bytes 393224 | tf_op jit(solution)/shard_map/ppermute | solution.py:14
where the time goes:
time: 90.9 us; the launch traced here: 90.6 us
  blocking collectives  39.1 us (43%)
  local copies, waits for them, and re-layouts  29.3 us (32%)
  other arithmetic  15.5 us (17%)
  waiting for transfers between devices  4.97 us (5%)
    all_to_all x1, blocking collectives, nearer_sums(): lax.all_to_all(stacked, 'los', split_axis=3, concat_axis=0, tiled=True)  21.6 us
    all_to_all x1, blocking collectives, nearer_sums(): lax.all_to_all(earlier, 'los', split_axis=0, concat_axis=3, tiled=True)  17.5 us
    unnamed x8, local copies, waits for them, and re-layouts  16.1 us
    all_to_all x2, local copies, waits for them, and re-layouts, nearer_sums(): lax.all_to_all(stacked, 'los', split_axis=3, concat_axis=0, tiled=True)  5.64 us
    ppermute x1, waiting for transfers between devices, with_halo(): lax.ppermute(tail, axis, [(i, (i + 1) % count) for i in range(count)])  4.96 us
    broadcast_in_dim x1, local copies, waits for them, and re-layouts, nearer_sums(): stacked = jnp.stack((total_near, total_far))[None]  4.39 us
    another operation x1, other arithmetic, nearer_sums(): earlier = jnp.cumsum(received, axis=0) - received  2.4 us
    div x1, other arithmetic, first_cols(): (jnp.roll(field, 2, axis=-1) - 8.0 * jnp.roll(field, 1, axis=-1) + 8.0 *...  2.3 us
  transfers between devices with their start and end apart: 2, of which 1 were waited for; matrix products, arithmetic and copies ran while one was open for 1% of the time, Pallas kernels for 0%

commit v1 on v0

v1 whole, which is shorter than its diff:
```python
import functools

import jax
import jax.numpy as jnp
from jax import lax
from jax.experimental import pallas as pl
from jax.experimental.pallas import tpu as pltpu
from jax.sharding import PartitionSpec as P

MESH = pl.DeviceIdType.MESH


def lens_kernel(
    los, sky, chunks, width, weight_ref, dist_ref, source_ref, pot_hbm,
    conv_ref, one_ref, two_ref,
    pot, edge_send, edge_recv, sent, own, got, sent_rim, own_rim, got_rim,
    before, before_rim, onward, onward_rim, back, back_rim,
    prefix, prefix_rim, rim_pot, lens,
    load_sem, edge_ssem, edge_rsem, x_ssem, x_rsem, z_ssem, z_rsem, b_ssem, b_rsem,
):
    f32 = jnp.float32
    shells, rows = pot.shape[0], pot.shape[1]
    half = chunks * width
    me = lax.axis_index("los")
    strip = lax.axis_index("sky")
    q = me // 2
    r = me % 2
    last = los // 2 - 1
    partner = me + 1 - 2 * r
    up = (strip + sky - 1) % sky
    down = (strip + 1) % sky

    load = pltpu.make_async_copy(pot_hbm, pot, load_sem)
    load.start()

    barrier = pltpu.get_barrier_semaphore()
    pl.semaphore_signal(barrier, inc=1, device_id={"los": partner}, device_id_type=MESH)
    pl.semaphore_signal(barrier, inc=1, device_id={"sky": up}, device_id_type=MESH)
    pl.semaphore_signal(barrier, inc=1, device_id={"sky": down}, device_id_type=MESH)

    @pl.when(q > 0)
    def _():
        pl.semaphore_signal(barrier, inc=1, device_id={"los": me - 2}, device_id_type=MESH)

    @pl.when(q < last)
    def _():
        pl.semaphore_signal(barrier, inc=1, device_id={"los": me + 2}, device_id_type=MESH)

    near = [weight_ref[j] * dist_ref[j] for j in range(shells)]
    far = [near[j] * dist_ref[j] for j in range(shells)]
    row = lax.broadcasted_iota(jnp.int32, (8, width), 0)

    load.wait()

    span = 2 * chunks
    for k in range(span):
        cols = pl.ds(k * width, width)
        top = jnp.zeros((8, width), f32)
        bottom = jnp.zeros((8, width), f32)
        for j in range(shells):
            block = pot[j, :, cols].astype(f32)
            mine = (row >= 2 * j) & (row < 2 * j + 2)
            head = block[:8]
            tail = block[rows - 8 :]
            top = jnp.where(mine, pltpu.roll(head, (2 * j) % 8, 0), top)
            bottom = jnp.where(mine, pltpu.roll(tail, (2 * j + 2) % 8, 0), bottom)
        edge_send[0, :, cols] = top.astype(jnp.bfloat16)
        edge_send[1, :, cols] = bottom.astype(jnp.bfloat16)

    peers = 3 + (q > 0).astype(jnp.int32) + (q < last).astype(jnp.int32)
    pl.semaphore_wait(barrier, peers)

    def remote(src, dst, ssem, rsem, **where):
        return pltpu.make_async_remote_copy(
            src_ref=src, dst_ref=dst, send_sem=ssem, recv_sem=rsem,
            device_id=where, device_id_type=MESH,
        )

    edges = [
        remote(edge_send.at[0], edge_recv.at[0], edge_ssem.at[0], edge_rsem.at[0], sky=up),
        remote(edge_send.at[1], edge_recv.at[1], edge_ssem.at[1], edge_rsem.at[1], sky=down),
    ]
    for copy in edges:
        copy.start()

    def totals(start):
        cols = pl.ds(pl.multiple_of(start, 128), width)
        total_near = jnp.zeros((rows, width), f32)
        total_far = jnp.zeros((rows, width), f32)
        for j in range(shells):
            block = pot[j, :, cols].astype(f32)
            total_near = total_near + near[j] * block
            total_far = total_far + far[j] * block
        return jnp.concatenate([total_near, total_far], axis=0)

    x_copies = [
        remote(sent.at[c], got.at[c], x_ssem.at[c], x_rsem.at[c], los=partner)
        for c in range(chunks)
    ] + [remote(sent_rim, got_rim, x_ssem.at[chunks], x_rsem.at[chunks], los=partner)]
    z_copies = [
        remote(onward.at[c], before.at[c], z_ssem.at[c], z_rsem.at[c], los=me + 2)
        for c in range(chunks)
    ] + [remote(onward_rim, before_rim, z_ssem.at[chunks], z_rsem.at[chunks], los=me + 2)]
    b_copies = [
        remote(back.at[c], prefix.at[r, c], b_ssem.at[c], b_rsem.at[c], los=partner)
        for c in range(chunks)
    ] + [remote(back_rim, prefix_rim.at[r], b_ssem.at[chunks], b_rsem.at[chunks], los=partner)]

    for c in range(chunks):
        sent[c] = totals((1 - r) * half + c * width)
        x_copies[c].start()
    for c in range(chunks):
        own[c] = totals(r * half + c * width)

    @pl.when(q == 0)
    def _():
        before[...] = jnp.zeros(before.shape, f32)
        before_rim[...] = jnp.zeros(before_rim.shape, f32)

    for copy in edges:
        copy.wait_recv()

    inner = (row >= 2) & (row < 6)
    for k in range(span):
        cols = pl.ds(k * width, width)
        below = edge_recv[0, :, cols].astype(f32)
        above = edge_recv[1, :, cols].astype(f32)
        total = jnp.zeros((8, width), f32)
        for j in range(shells):
            tile = jnp.where(
                row < 2,
                pltpu.roll(below, (8 - 2 * j) % 8, 0),
                jnp.where(
                    row < 4,
                    pltpu.roll(below, (10 - 2 * j) % 8, 0),
                    jnp.where(
                        row < 6,
                        pltpu.roll(above, (12 - 2 * j) % 8, 0),
                        pltpu.roll(above, (14 - 2 * j) % 8, 0),
                    ),
                ),
            )
            scaled = tile * jnp.where(inner, far[j], near[j])
            rim_pot[j, k] = scaled
            total = total + scaled
        own_rim[k // chunks, k % chunks] = total
    sent_rim[...] = own_rim[1 - r]
    x_copies[chunks].start()

    is_odd = r.astype(f32)
    is_even = 1.0 - is_odd

    for c in range(chunks + 1):
        x_copies[c].wait_recv()

        @pl.when(q > 0)
        def _():
            z_copies[c].wait_recv()

        if c < chunks:
            mine, other, base = own[c], got[c], before[c]
            next_ref, back_ref, keep_ref = onward.at[c], back.at[c], prefix.at[r, c]
        else:
            mine, other, base = own_rim[r], got_rim[...], before_rim[...]
            next_ref, back_ref, keep_ref = onward_rim, back_rim, prefix_rim.at[r]
        next_ref[...] = base + (mine + other)

        @pl.when(q < last)
        def _():
            z_copies[c].start()

        back_ref[...] = base + is_even * mine
        b_copies[c].start()
        keep_ref[...] = base + is_odd * other

    for c in range(chunks + 1):
        b_copies[c].wait_recv()

    inverse = [1.0 / jnp.full((8, width), source_ref[j], f32) for j in range(shells)]

    def lens_chunk(k, carry):
        cols = pl.ds(pl.multiple_of(k * width, 128), width)
        part, c = k // chunks, k % chunks
        sums = prefix[part, c]
        run_near, run_far = sums[:rows], sums[rows:]
        rim = prefix_rim[part, c]
        for j in range(shells):
            block = pot[j, :, cols].astype(f32)
            run_near = run_near + near[j] * block
            run_far = run_far + far[j] * block
            rim = rim + rim_pot[j, k]
            far_rim = jnp.where(row < 4, pltpu.roll(rim, 6, 0), pltpu.roll(rim, 2, 0))
            scale = jnp.concatenate([inverse[j]] * (rows // 8), axis=0)
            lens[j, k, :rows] = run_near - run_far * scale
            lens[j, k, rows:] = rim - far_rim * inverse[j]
        return carry

    lax.fori_loop(0, span, lens_chunk, 0)

    def stencil_chunk(k, carry):
        cols = pl.ds(pl.multiple_of(k * width, 128), width)
        before_k = (k + span - 1) % span
        after_k = (k + 1) % span
        for j in range(shells):
            centre = lens[j, k]
            wide = jnp.concatenate(
                [lens[j, before_k, :, width - 128 :], centre, lens[j, after_k, :, :128]], axis=1
            )
            full = width + 256

            def shift(n):
                return pltpu.roll(wide, n % full, 1)[:, 128 : 128 + width]

            left1, right1, left2, right2 = shift(1), shift(-1), shift(2), shift(-2)
            slope = (left2 - right2) + 8.0 * (right1 - left1)
            second_x = (16.0 * (left1 + right1) - (left2 + right2))[:rows]

            def rows_at(field, n):
                return pltpu.roll(field, (-n) % (rows + 8), 0)[:rows]

            second_y = 16.0 * (rows_at(centre, -1) + rows_at(centre, 1)) - (
                rows_at(centre, -2) + rows_at(centre, 2)
            )
            cross = (rows_at(slope, -2) - rows_at(slope, 2)) + 8.0 * (
                rows_at(slope, 1) - rows_at(slope, -1)
            )
            middle = 60.0 * centre[:rows]
            conv_ref[j, :, cols] = ((second_x + second_y - middle) * (1.0 / 24.0)).astype(jnp.bfloat16)
            one_ref[j, :, cols] = ((second_x - second_y) * (1.0 / 24.0)).astype(jnp.bfloat16)
            two_ref[j, :, cols] = (cross * (1.0 / 144.0)).astype(jnp.bfloat16)
        return carry

    lax.fori_loop(0, span, stencil_chunk, 0)

    for copy in edges:
        copy.wait_send()
    for c in range(chunks + 1):
        x_copies[c].wait_send()
        b_copies[c].wait_send()

    @pl.when(q < last)
    def _():
        for c in range(chunks + 1):
            z_copies[c].wait_send()


def on_device(los, sky, potentials, shell_weight, shell_dist, source_dist):
    shells, rows, ncols = potentials.shape
    half = ncols // 2
    chunks = next(n for n in (8, 4, 2, 1) if half % (n * 128) == 0)
    width = half // chunks
    f32, bf16 = jnp.float32, jnp.bfloat16
    dma = pltpu.SemaphoreType.DMA
    smem = pl.BlockSpec(memory_space=pltpu.SMEM)
    vmem = pl.BlockSpec(memory_space=pltpu.VMEM)
    main = (chunks, 2 * rows, width)
    rim = (chunks, 8, width)
    return tuple(pl.pallas_call(
        functools.partial(lens_kernel, los, sky, chunks, width),
        out_shape=[jax.ShapeDtypeStruct(potentials.shape, bf16)] * 3,
        in_specs=[smem, smem, smem, pl.BlockSpec(memory_space=pl.ANY)],
        out_specs=[vmem] * 3,
        scratch_shapes=[
            pltpu.VMEM(potentials.shape, bf16),
            pltpu.VMEM((2, 8, ncols), bf16),
            pltpu.VMEM((2, 8, ncols), bf16),
            pltpu.VMEM(main, f32),
            pltpu.VMEM(main, f32),
            pltpu.VMEM(main, f32),
            pltpu.VMEM(rim, f32),
            pltpu.VMEM((2,) + rim, f32),
            pltpu.VMEM(rim, f32),
            pltpu.VMEM(main, f32),
            pltpu.VMEM(rim, f32),
            pltpu.VMEM(main, f32),
            pltpu.VMEM(rim, f32),
            pltpu.VMEM(main, f32),
            pltpu.VMEM(rim, f32),
            pltpu.VMEM((2,) + main, f32),
            pltpu.VMEM((2,) + rim, f32),
            pltpu.VMEM((shells, 2 * chunks, 8, width), f32),
            pltpu.VMEM((shells, 2 * chunks, rows + 8, width), f32),
            dma,
            dma((2,)),
            dma((2,)),
            dma((chunks + 1,)),
            dma((chunks + 1,)),
            dma((chunks + 1,)),
            dma((chunks + 1,)),
            dma((chunks + 1,)),
            dma((chunks + 1,)),
        ],
        compiler_params=pltpu.CompilerParams(collective_id=0, has_side_effects=True),
    )(shell_weight, shell_dist, source_dist, potentials))


def solution(mesh):
    return jax.shard_map(
        functools.partial(on_device, mesh.shape["los"], mesh.shape["sky"]),
        mesh=mesh,
        in_specs=(P("los", "sky", None), P("los"), P("los"), P("los")),
        out_specs=(P("los", "sky", None), P("los", "sky", None), P("los", "sky", None)),
        check_vma=False,
    )
```

time: 90.9 us -> 34.3 us (0.38)
  the two profiles are of different devices: /device:TPU:0 before, /device:TPU:24 now
where the time goes in v1:
time: 34.3 us; the launch traced here: 34 us
  Pallas kernels  29.4 us (86%)
  local copies, waits for them, and re-layouts  3.95 us (12%)
  between operations  0.65 us (2%)
    pallas_call x1, Pallas kernels, on_device(): pl.pallas_call(functools.partial(lens_kernel, los, sky, chunks, width), o...  29.4 us
    unnamed x7, local copies, waits for them, and re-layouts  3.95 us

profile of v1, /device:TPU:24, one launch (start us, length us, event | category | flops | bytes accessed | tf_op | source)
XLA Modules:
  0.0 34.0 jit_solution(3351857577287261987)
XLA Ops:
  0.6 29.4 %shard_map.67 = (bf16[4,16,4096]{2,1,0:T(8,128)(2,1)}, bf16[4,16,4096]{2,1,0:T(8,128)(2,1)}, bf16[4,16,4096]{2,1,0:T(8,128)(2,1)}) custom-call(f32[4]{0:T(128)} %weight_ref.1, f32[4]{0:T(128)} %dist_ref.1, f32[4]{0:T(128)} %source_ref.1, bf16[4,16,4096]{2,1,0:T(8,128)(2,1)} %pot_hbm.1), custom_call_target="tpu_custom_call" | custom-call | tf_op jit(solution)/shard_map/pallas_call | solution.py:258
  30.0 0.0 copy-start.1
  30.1 1.9 %copy.10 = bf16[4,16,4096]{2,1,0:T(8,128)(2,1)} copy(bf16[4,16,4096]{2,1,0:T(8,128)(2,1)} %get-tuple-element.6) | data formatting | bytes 1048576
  32.0 0.0 copy-done.1
  32.0 0.0 copy-start
  32.0 0.8 %copy.11 = bf16[4,16,4096]{2,1,0:T(8,128)(2,1)} copy(bf16[4,16,4096]{2,1,0:T(8,128)(2,1)S(1)} %copy-done.1) | data formatting | bytes 1048576
  32.8 0.4 %copy-done = bf16[4,16,4096]{2,1,0:T(8,128)(2,1)S(1)} copy-done((bf16[4,16,4096]{2,1,0:T(8,128)(2,1)S(1)}, bf16[4,16,4096]{2,1,0:T(8,128)(2,1)}, u32[]{:S(2)}) %copy-start) | copy-done | bytes 524312
  33.2 0.8 %copy.12 = bf16[4,16,4096]{2,1,0:T(8,128)(2,1)} copy(bf16[4,16,4096]{2,1,0:T(8,128)(2,1)S(1)} %copy-done) | data formatting | bytes 1048576
Async XLA Ops:
  30.0 1.9 %copy-start.1 = (bf16[4,16,4096]{2,1,0:T(8,128)(2,1)S(1)}, bf16[4,16,4096]{2,1,0:T(8,128)(2,1)}, u32[]{:S(2)}) copy-start(bf16[4,16,4096]{2,1,0:T(8,128)(2,1)} %get-tuple-element.7) | copy-start | bytes 1572868
  32.0 1.2 %copy-start = (bf16[4,16,4096]{2,1,0:T(8,128)(2,1)S(1)}, bf16[4,16,4096]{2,1,0:T(8,128)(2,1)}, u32[]{:S(2)}) copy-start(bf16[4,16,4096]{2,1,0:T(8,128)(2,1)} %get-tuple-element.8) | copy-start | bytes 1572868

commit v2 on v1

--- a/solution.py
+++ b/solution.py
@@ -30,8 +30,15 @@
     up = (strip + sky - 1) % sky
     down = (strip + 1) % sky
 
-    load = pltpu.make_async_copy(pot_hbm, pot, load_sem)
-    load.start()
+    span = 2 * chunks
+    loads = []
+    for c in range(span):
+        part = (1 - r) if c < chunks else r
+        cols = pl.ds(pl.multiple_of((part * chunks + c % chunks) * width, 128), width)
+        loads.append(
+            pltpu.make_async_copy(pot_hbm.at[:, :, cols], pot.at[:, :, cols], load_sem.at[c])
+        )
+        loads[-1].start()
 
     barrier = pltpu.get_barrier_semaphore()
     pl.semaphore_signal(barrier, inc=1, device_id={"los": partner}, device_id_type=MESH)
@@ -50,9 +57,55 @@
     far = [near[j] * dist_ref[j] for j in range(shells)]
     row = lax.broadcasted_iota(jnp.int32, (8, width), 0)
 
-    load.wait()
-
-    span = 2 * chunks
+    def totals(start):
+        cols = pl.ds(pl.multiple_of(start, 128), width)
+        total_near = jnp.zeros((rows, width), f32)
+        total_far = jnp.zeros((rows, width), f32)
+        for j in range(shells):
+            block = pot[j, :, cols].astype(f32)
+            total_near = total_near + near[j] * block
+            total_far = total_far + far[j] * block
+        return jnp.concatenate([total_near, total_far], axis=0)
+
+    def remote(src, dst, ssem, rsem, **where):
+        return pltpu.make_async_remote_copy(
+            src_ref=src, dst_ref=dst, send_sem=ssem, recv_sem=rsem,
+            device_id=where, device_id_type=MESH,
+        )
+
+    x_copies = [
+        remote(sent.at[c], got.at[c], x_ssem.at[c], x_rsem.at[c], los=partner)
+        for c in range(chunks)
+    ] + [remote(sent_rim, got_rim, x_ssem.at[chunks], x_rsem.at[chunks], los=partner)]
+    z_copies = [
+        remote(onward.at[c], before.at[c], z_ssem.at[c], z_rsem.at[c], los=me + 2)
+        for c in range(chunks)
+    ] + [remote(onward_rim, before_rim, z_ssem.at[chunks], z_rsem.at[chunks], los=me + 2)]
+    b_copies = [
+        remote(back.at[c], prefix.at[r, c], b_ssem.at[c], b_rsem.at[c], los=partner)
+        for c in range(chunks)
+    ] + [remote(back_rim, prefix_rim.at[r], b_ssem.at[chunks], b_rsem.at[chunks], los=partner)]
+
+    edges = [
+        remote(edge_send.at[0], edge_recv.at[0], edge_ssem.at[0], edge_rsem.at[0], sky=up),
+        remote(edge_send.at[1], edge_recv.at[1], edge_ssem.at[1], edge_rsem.at[1], sky=down),
+    ]
+    rim_at = max(1, chunks * 5 // 8)
+
+    def send_totals(c):
+        sent[c] = totals((1 - r) * half + c * width)
+        x_copies[c].start()
+
+    loads[0].wait()
+    sent[0] = totals((1 - r) * half)
+
+    peers = 3 + (q > 0).astype(jnp.int32) + (q < last).astype(jnp.int32)
+    pl.semaphore_wait(barrier, peers)
+
+    x_copies[0].start()
+    for copy in loads[1:]:
+        copy.wait()
+
     for k in range(span):
         cols = pl.ds(k * width, width)
         top = jnp.zeros((8, width), f32)
@@ -67,48 +120,10 @@
         edge_send[0, :, cols] = top.astype(jnp.bfloat16)
         edge_send[1, :, cols] = bottom.astype(jnp.bfloat16)
 
-    peers = 3 + (q > 0).astype(jnp.int32) + (q < last).astype(jnp.int32)
-    pl.semaphore_wait(barrier, peers)
-
-    def remote(src, dst, ssem, rsem, **where):
-        return pltpu.make_async_remote_copy(
-            src_ref=src, dst_ref=dst, send_sem=ssem, recv_sem=rsem,
-            device_id=where, device_id_type=MESH,
-        )
-
-    edges = [
-        remote(edge_send.at[0], edge_recv.at[0], edge_ssem.at[0], edge_rsem.at[0], sky=up),
-        remote(edge_send.at[1], edge_recv.at[1], edge_ssem.at[1], edge_rsem.at[1], sky=down),
-    ]
     for copy in edges:
         copy.start()
-
-    def totals(start):
-        cols = pl.ds(pl.multiple_of(start, 128), width)
-        total_near = jnp.zeros((rows, width), f32)
-        total_far = jnp.zeros((rows, width), f32)
-        for j in range(shells):
-            block = pot[j, :, cols].astype(f32)
-            total_near = total_near + near[j] * block
-            total_far = total_far + far[j] * block
-        return jnp.concatenate([total_near, total_far], axis=0)
-
-    x_copies = [
-        remote(sent.at[c], got.at[c], x_ssem.at[c], x_rsem.at[c], los=partner)
-        for c in range(chunks)
-    ] + [remote(sent_rim, got_rim, x_ssem.at[chunks], x_rsem.at[chunks], los=partner)]
-    z_copies = [
-        remote(onward.at[c], before.at[c], z_ssem.at[c], z_rsem.at[c], los=me + 2)
-        for c in range(chunks)
-    ] + [remote(onward_rim, before_rim, z_ssem.at[chunks], z_rsem.at[chunks], los=me + 2)]
-    b_copies = [
-        remote(back.at[c], prefix.at[r, c], b_ssem.at[c], b_rsem.at[c], los=partner)
-        for c in range(chunks)
-    ] + [remote(back_rim, prefix_rim.at[r], b_ssem.at[chunks], b_rsem.at[chunks], los=partner)]
-
-    for c in range(chunks):
-        sent[c] = totals((1 - r) * half + c * width)
-        x_copies[c].start()
+    for c in range(1, rim_at):
+        send_totals(c)
     for c in range(chunks):
         own[c] = totals(r * half + c * width)
 
@@ -147,10 +162,13 @@
     sent_rim[...] = own_rim[1 - r]
     x_copies[chunks].start()
 
+    for c in range(rim_at, chunks):
+        send_totals(c)
+
     is_odd = r.astype(f32)
     is_even = 1.0 - is_odd
 
-    for c in range(chunks + 1):
+    def forward(c):
         x_copies[c].wait_recv()
 
         @pl.when(q > 0)
@@ -173,12 +191,10 @@
         b_copies[c].start()
         keep_ref[...] = base + is_odd * other
 
-    for c in range(chunks + 1):
-        b_copies[c].wait_recv()
-
     inverse = [1.0 / jnp.full((8, width), source_ref[j], f32) for j in range(shells)]
 
-    def lens_chunk(k, carry):
+    def lens_chunk(place, carry):
+        k = (r * chunks + place) % span
         cols = pl.ds(pl.multiple_of(k * width, 128), width)
         part, c = k // chunks, k % chunks
         sums = prefix[part, c]
@@ -195,9 +211,8 @@
             lens[j, k, rows:] = rim - far_rim * inverse[j]
         return carry
 
-    lax.fori_loop(0, span, lens_chunk, 0)
-
-    def stencil_chunk(k, carry):
+    def stencil_chunk(place, carry):
+        k = (r * chunks + place) % span
         cols = pl.ds(pl.multiple_of(k * width, 128), width)
         before_k = (k + span - 1) % span
         after_k = (k + 1) % span
@@ -230,7 +245,72 @@
             two_ref[j, :, cols] = (cross * (1.0 / 144.0)).astype(jnp.bfloat16)
         return carry
 
-    lax.fori_loop(0, span, stencil_chunk, 0)
+    order = list(range(rim_at)) + [chunks] + list(range(rim_at, chunks))
+
+    @pl.when(q < last)
+    def _():
+        for c in order:
+            forward(c)
+        lax.fori_loop(0, chunks, lens_chunk, 0)
+        lax.fori_loop(1, chunks - 1, stencil_chunk, 0)
+        for c in order:
+            b_copies[c].wait_recv()
+        lax.fori_loop(chunks, span, lens_chunk, 0)
+        lax.fori_loop(chunks - 1, span + 1, stencil_chunk, 0)
+
+    @pl.when(q == last)
+    def _():
+        arrived, mapped, done = set(), set(), set()
+
+        def run(body, places):
+            while places:
+                count = 1
+                while count < len(places) and places[count] == places[0] + count:
+                    count += 1
+                lax.fori_loop(places[0], places[0] + count, body, 0)
+                places = places[count:]
+
+        def advance(limit):
+            ready = []
+            for place in sorted(arrived - mapped):
+                rim_place = "own" if place < chunks else "other"
+                if rim_place in rims:
+                    ready.append(place)
+            run(lens_chunk, ready)
+            mapped.update(ready)
+            ready = [
+                place
+                for place in range(span)
+                if place not in done
+                and {(place - 1) % span, place, (place + 1) % span} <= mapped
+            ][:limit]
+            run(stencil_chunk, ready)
+            done.update(ready)
+
+        rims = set()
+
+        def receive(c):
+            b_copies[c].wait_recv()
+            if c == chunks:
+                rims.add("other")
+            else:
+                arrived.add(chunks + c)
+
+        waited = 0
+        for n, c in enumerate(order):
+            forward(c)
+            if c == chunks:
+                rims.add("own")
+            else:
+                arrived.add(c)
+            if "own" in rims and n > rim_at:
+                while waited < n - 1:
+                    receive(order[waited])
+                    waited += 1
+            advance(4)
+        for c in order[waited:]:
+            receive(c)
+            advance(span)
 
     for copy in edges:
         copy.wait_send()
@@ -242,6 +322,18 @@
     def _():
         for c in range(chunks + 1):
             z_copies[c].wait_send()
+
+
+def store_kernel(a, b, c, to_a, to_b, to_c, sems):
+    copies = [
+        pltpu.make_async_copy(src.at[j], dst.at[j], sems.at[n, j])
+        for n, (src, dst) in enumerate(((a, to_a), (b, to_b), (c, to_c)))
+        for j in range(a.shape[0])
+    ]
+    for copy in copies:
+        copy.start()
+    for copy in copies:
+        copy.wait()
 
 
 def on_device(los, sky, potentials, shell_weight, shell_dist, source_dist):
@@ -255,9 +347,9 @@
     vmem = pl.BlockSpec(memory_space=pltpu.VMEM)
     main = (chunks, 2 * rows, width)
     rim = (chunks, 8, width)
-    return tuple(pl.pallas_call(
+    staged = pl.pallas_call(
         functools.partial(lens_kernel, los, sky, chunks, width),
-        out_shape=[jax.ShapeDtypeStruct(potentials.shape, bf16)] * 3,
+        out_shape=[pltpu.VMEM(potentials.shape, bf16)] * 3,
         in_specs=[smem, smem, smem, pl.BlockSpec(memory_space=pl.ANY)],
         out_specs=[vmem] * 3,
         scratch_shapes=[
@@ -280,7 +372,7 @@
             pltpu.VMEM((2,) + rim, f32),
             pltpu.VMEM((shells, 2 * chunks, 8, width), f32),
             pltpu.VMEM((shells, 2 * chunks, rows + 8, width), f32),
-            dma,
+            dma((2 * chunks,)),
             dma((2,)),
             dma((2,)),
             dma((chunks + 1,)),
@@ -291,7 +383,15 @@
             dma((chunks + 1,)),
         ],
         compiler_params=pltpu.CompilerParams(collective_id=0, has_side_effects=True),
-    )(shell_weight, shell_dist, source_dist, potentials))
+    )(shell_weight, shell_dist, source_dist, potentials)
+    anywhere = pl.BlockSpec(memory_space=pl.ANY)
+    return tuple(pl.pallas_call(
+        store_kernel,
+        out_shape=[jax.ShapeDtypeStruct(potentials.shape, bf16)] * 3,
+        in_specs=[vmem] * 3,
+        out_specs=[anywhere] * 3,
+        scratch_shapes=[dma((3, shells))],
+    )(*[pltpu.with_memory_space_constraint(x, pltpu.VMEM) for x in staged]))
 
 
 def solution(mesh):

time: 34.3 us -> 30.1 us (0.88)
  local copies, waits for them, and re-layouts: 3.95 us -> 0 us
    unnamed x7 -> x0, local copies, waits for them, and re-layouts: 3.95 us -> none
    pallas_call x1, Pallas kernels: 29.4 us -> 28.1 us  [on_device(): pl.pallas_call(functools.partial(lens_kernel, los, sky, chunks, width), o...]
    pallas_call x0 -> x1, Pallas kernels: none -> 1.24 us  [on_device(): pl.pallas_call(store_kernel, out_shape=[jax.ShapeDtypeStruct(potentials.s...]
where the time goes in v2:
time: 30.1 us; the launch traced here: 29.9 us
  Pallas kernels  29.3 us (97%)
  between operations  0.64 us (2%)
    pallas_call x1, Pallas kernels, on_device(): pl.pallas_call(functools.partial(lens_kernel, los, sky, chunks, width), o...  28.1 us
    pallas_call x1, Pallas kernels, on_device(): pl.pallas_call(store_kernel, out_shape=[jax.ShapeDtypeStruct(potentials.s...  1.24 us

profile of v2, /device:TPU:24, one launch (start us, length us, event | category | flops | bytes accessed | tf_op | source)
XLA Modules:
  0.0 29.9 jit_solution(6404615549236581326)
XLA Ops:
  0.6 28.1 %shard_map.67 = (bf16[4,16,4096]{2,1,0:T(8,128)(2,1)S(1)}, bf16[4,16,4096]{2,1,0:T(8,128)(2,1)S(1)}, bf16[4,16,4096]{2,1,0:T(8,128)(2,1)S(1)}) custom-call(f32[4]{0:T(128)} %weight_ref.1, f32[4]{0:T(128)} %dist_ref.1, f32[4]{0:T(128)} %source_ref.1, bf16[4,16,4096]{2,1,0:T(8,128)(2,1)} %pot_hbm.1), custom_call_target="tpu_custom_call" | custom-call | tf_op jit(solution)/shard_map/pallas_call | solution.py:350
  28.7 1.2 %shard_map.68 = (bf16[4,16,4096]{2,1,0:T(8,128)(2,1)}, bf16[4,16,4096]{2,1,0:T(8,128)(2,1)}, bf16[4,16,4096]{2,1,0:T(8,128)(2,1)}) custom-call(bf16[4,16,4096]{2,1,0:T(8,128)(2,1)S(1)} %get-tuple-element.6.a, bf16[4,16,4096]{2,1,0:T(8,128)(2,1)S(1)} %get-tuple-element.7.b, bf16[4,16,4096]{2,1,0:T(8,128)(2,1)S(1)} %get-tuple-element.8.c), custom_call_target="tpu_custom_call" | custom-call | tf_op jit(solution)/shard_map/pallas_call | solution.py:388

commit v3 on v2

--- a/solution.py
+++ b/solution.py
@@ -339,7 +339,7 @@
 def on_device(los, sky, potentials, shell_weight, shell_dist, source_dist):
     shells, rows, ncols = potentials.shape
     half = ncols // 2
-    chunks = next(n for n in (8, 4, 2, 1) if half % (n * 128) == 0)
+    chunks = next(n for n in (4, 2, 1) if half % (n * 128) == 0)
     width = half // chunks
     f32, bf16 = jnp.float32, jnp.bfloat16
     dma = pltpu.SemaphoreType.DMA

time: 30.1 us -> 27.9 us (0.927)
  Pallas kernels: 29.3 us -> 27.1 us
    pallas_call x1, Pallas kernels: 28.1 us -> 25.8 us  [on_device(): pl.pallas_call(functools.partial(lens_kernel, los, sky, chunks, width), o...]
where the time goes in v3:
time: 27.9 us; the launch traced here: 27.7 us
  Pallas kernels  27.1 us (97%)
  between operations  0.64 us (2%)
    pallas_call x1, Pallas kernels, on_device(): pl.pallas_call(functools.partial(lens_kernel, los, sky, chunks, width), o...  25.8 us
    pallas_call x1, Pallas kernels, on_device(): pl.pallas_call(store_kernel, out_shape=[jax.ShapeDtypeStruct(potentials.s...  1.24 us

profile of v3, /device:TPU:24, one launch (start us, length us, event | category | flops | bytes accessed | tf_op | source)
XLA Modules:
  0.0 27.7 jit_solution(14961766212421034836)
XLA Ops:
  0.6 25.8 %shard_map.67 = (bf16[4,16,4096]{2,1,0:T(8,128)(2,1)S(1)}, bf16[4,16,4096]{2,1,0:T(8,128)(2,1)S(1)}, bf16[4,16,4096]{2,1,0:T(8,128)(2,1)S(1)}) custom-call(f32[4]{0:T(128)} %weight_ref.1, f32[4]{0:T(128)} %dist_ref.1, f32[4]{0:T(128)} %source_ref.1, bf16[4,16,4096]{2,1,0:T(8,128)(2,1)} %pot_hbm.1), custom_call_target="tpu_custom_call" | custom-call | tf_op jit(solution)/shard_map/pallas_call | solution.py:350
  26.5 1.2 %shard_map.68 = (bf16[4,16,4096]{2,1,0:T(8,128)(2,1)}, bf16[4,16,4096]{2,1,0:T(8,128)(2,1)}, bf16[4,16,4096]{2,1,0:T(8,128)(2,1)}) custom-call(bf16[4,16,4096]{2,1,0:T(8,128)(2,1)S(1)} %get-tuple-element.6.a, bf16[4,16,4096]{2,1,0:T(8,128)(2,1)S(1)} %get-tuple-element.7.b, bf16[4,16,4096]{2,1,0:T(8,128)(2,1)S(1)} %get-tuple-element.8.c), custom_call_target="tpu_custom_call" | custom-call | tf_op jit(solution)/shard_map/pallas_call | solution.py:388
